TPU v7x, 256 devices: a whole 4x4x8 slice. The times are simulated.
256 devices in a mesh: fsdp: 16 (over z_hi, x), tensor: 4 (over z_lo, core), replica: 4 (over y).
Axes of the slice: x: 4, y: 4, z: 8 (z_hi: 4, z_lo: 2; z = z_hi * 2 + z_lo), core: 2. Of those that a mesh axis runs over, the one named last changes fastest.
Arguments:
- activations: bfloat16 [24576, 8192], P(('fsdp', 'replica'))
- norm_gain: float32 [8192], replicated, may hold values from 0.1 to 1.9
- key_weight: bfloat16 [8192, 1024], P('fsdp', 'tensor'), may hold values from -0.0625 to 0.0625
- value_weight: bfloat16 [8192, 1024], P('fsdp', 'tensor'), may hold values from -0.0625 to 0.0625
- key_cot: bfloat16 [24576, 1024], P(('fsdp', 'replica'), 'tensor'), may hold values from -6 to 6
- value_cot: bfloat16 [24576, 1024], P(('fsdp', 'replica'), 'tensor'), may hold values from -6 to 6
- blocks: int32 [2, 64, 2], P(None, 'tensor'), may hold values from 0 to 127, as said below
Outputs:
- key_out: bfloat16 [24576, 1024], P(('fsdp', 'replica'), 'tensor')
- value_out: bfloat16 [24576, 1024], P(('fsdp', 'replica'), 'tensor')
- normed_grad: bfloat16 [24576, 8192], P(('fsdp', 'replica'), 'tensor')
- block_grads: float32 [2, 64, 4096], P(None, 'tensor')
Inputs may be any that keep to these rules, and one draw needn't show every extreme that they name: Each run of 16 entries of one projection names 16 distinct blocks of one tensor shard, as (row block below 128, column block below the shard's key columns / 64).
All inputs are finite; a program needn't handle non-finite values.
Results may differ from a plain program's by a relative error of at most 0.013.
Values may be sent and summed in bfloat16 or wider, within the bound.
A program may use at most 128 MiB of HBM per device.

v0:
```python
import jax
import jax.numpy as jnp
from jax import lax
from jax.sharding import PartitionSpec as P

D = 8192
BLK = 64
norm_epsilon = 1e-05


def local(activations, norm_gain, key_weight, value_weight, key_cot, value_cot, blocks):
    tok_rows = activations.shape[0]
    shard_width = key_weight.shape[1]
    widened = activations.astype(jnp.float32)
    inverse_rms = lax.rsqrt(jnp.mean(widened * widened, axis=1, keepdims=True) + norm_epsilon)
    normed = (widened * inverse_rms * norm_gain).astype(jnp.bfloat16)
    stacked = jnp.concatenate([key_weight, value_weight], axis=1)
    cot_both = jnp.concatenate([key_cot, value_cot], axis=1)
    contract_cols = (((1,), (1,)), ((), ()))
    shard_rows = lax.all_gather(stacked, "fsdp", axis=0, tiled=True)
    running = jnp.dot(normed, shard_rows, preferred_element_type=jnp.float32)
    whole = shard_rows
    running, whole = (running, whole)
    partial_value = lax.dot_general(
        cot_both, whole, contract_cols, preferred_element_type=jnp.float32
    ).astype(jnp.bfloat16)
    key_out = running[:, :shard_width].astype(jnp.bfloat16)
    value_out = running[:, shard_width:].astype(jnp.bfloat16)
    normed_grad = (
        lax.psum_scatter(partial_value, "tensor", scatter_dimension=1, tiled=True)
        .astype(jnp.float32)
        .astype(jnp.bfloat16)
    )
    row_index = blocks[:, :, 0].reshape(-1)
    column_index = blocks[:, :, 1]
    left_blocks = jnp.take(normed.reshape(tok_rows, D // BLK, BLK), row_index, axis=1)
    key_blocks = jnp.take(
        key_cot.reshape(tok_rows, shard_width // BLK, BLK), column_index[0], axis=1
    )
    value_blocks = jnp.take(
        value_cot.reshape(tok_rows, shard_width // BLK, BLK), column_index[1], axis=1
    )
    right_blocks = jnp.concatenate([key_blocks, value_blocks], axis=1)
    local_grads = jnp.einsum(
        "tbi,tbj->bij", left_blocks, right_blocks, preferred_element_type=jnp.float32
    )
    local_grads = local_grads.reshape(2, blocks.shape[1], BLK * BLK)
    block_grads = lax.psum(local_grads, ("fsdp", "replica"))
    return (key_out, value_out, normed_grad, block_grads)


def solution(mesh):
    in_specs = (
        P(("fsdp", "replica"), None),
        P(),
        P("fsdp", "tensor"),
        P("fsdp", "tensor"),
        P(("fsdp", "replica"), "tensor"),
        P(("fsdp", "replica"), "tensor"),
        P(None, "tensor", None),
    )
    out_specs = (
        P(("fsdp", "replica"), "tensor"),
        P(("fsdp", "replica"), "tensor"),
        P(("fsdp", "replica"), "tensor"),
        P(None, "tensor", None),
    )
    return jax.shard_map(local, mesh=mesh, in_specs=in_specs, out_specs=out_specs, check_vma=False)
```

profile of v0, /device:TPU:8, one launch (start us, length us, event | category | flops | bytes accessed | tf_op | source)
XLA Modules:
  0.0 862.2 jit_solution(1816326400129489290)
XLA Ops:
  8.0 0.0 all-gather.2.cloned.1.call-start
  8.0 1.9 pad_maximum_fusion
  9.9 0.0 all-gather.2.cloned.1.call-update
  9.9 0.0 all-reduce.2.cloned.1.call-start
  10.0 1.1 copy.12
  11.1 1.1 copy.13
  12.2 0.0 copy-start.2
  12.2 8.7 %copy.11 = bf16[384,8192]{0,1:T(8,128)(2,1)} copy(bf16[384,8192]{1,0:T(8,128)(2,1)} %param.9) | data formatting | bytes 12582912 | tf_op args[0]
  20.9 0.0 copy-done.2
  20.9 0.1 reshape_squeeze.6
  21.0 0.1 reshape_squeeze.5
  21.1 0.0 copy-start.1
  21.1 0.7 gather_fusion.1
  21.8 0.7 gather_fusion.2
  22.6 4.2 fusion
  26.8 0.0 copy-done.1
  26.8 8.2 fusion.2
  35.0 3.8 gather_fusion
  38.7 0.0 copy-start
  38.8 0.2 select_bitcast_fusion
  39.0 0.8 fusion.3
  39.8 1.2 reshape.75
  41.0 0.0 all-reduce.2.cloned.1.call-update
  41.0 0.0 reduce-scatter.2.cloned.1.call-start
  41.0 77.6 %all-gather.2.cloned.1.call-done = bf16[8192,512]{1,0:T(8,128)(2,1)} async-done(((bf16[512,512]{1,0:T(8,128)(2,1)}), bf16[8192,512]{1,0:T(8,128)(2,1)}) %all-gather.2.cloned.1.call-update) | async-done | bytes 8388624 | tf_op jit(solution)/shard_map/all_gather | solution.py:20
  118.6 0.0 copy-done
  118.6 9.7 %convolution_convert_fusion = bf16[384,8192]{1,0:T(8,128)(2,1)} fusion(bf16[8192,512]{1,0:T(8,128)(2,1)} %all-gather.2.cloned.1.call-done, bf16[384,256]{1,0:T(8,128)(2,1)S(1)} %copy-done, bf16[384,256]{1,0:T(8,128)(2,1)} %param.13), kind=kOutput, calls=%fused_computation.8 | convolution fusion | flops 3225157632 | bytes 15073280 | tf_op jit(solution)/shard_map/dot_general | solution.py:24
  128.3 0.0 reduce-scatter.2.cloned.1.call-update
  128.3 8.6 %convolution_convert_fusion.1 = bf16[384,512]{1,0:T(8,128)(2,1)S(1)} fusion(bf16[384,8192]{0,1:T(8,128)(2,1)} %fusion.2, bf16[8192,512]{1,0:T(8,128)(2,1)} %all-gather.2.cloned.1.call-done), kind=kOutput, calls=%fused_computation.16 | convolution fusion | flops 3221422080 | bytes 15073280 | tf_op jit(solution)/shard_map/dot_general | solution.py:21
  136.9 0.8 fusion.18
  137.7 715.1 %all-reduce.2.cloned.1.call-done = f32[2,16,4096]{2,1,0:T(8,128)} async-done(((f32[2,16,4096]{2,1,0:T(8,128)}), f32[2,16,4096]{2,1,0:T(8,128)}) %all-reduce.2.cloned.1.call-update) | async-done | bytes 524304 | tf_op jit(solution)/shard_map/psum | solution.py:48
  852.9 1.9 copy.15
  (9 shorter events, 0.1 us)
Async XLA Ops:
  8.0 110.6 %all-gather.2.cloned.1.call-start = ((), (), s32[]{:S(2)}) async-start(), calls=%async_computation.1 | async-start | bytes 8912896 | tf_op jit(solution)/shard_map/all_gather | solution.py:20
  9.9 842.9 %all-reduce.2.cloned.1.call-start = ((), (), s32[]{:S(2)}) async-start(), calls=%async_computation.3 | async-start | bytes 1048576 | tf_op jit(solution)/shard_map/psum | solution.py:48
  12.2 8.7 %copy-start.2 = (s32[2,16,2]{1,2,0:T(2,128)S(1)}, s32[2,16,2]{1,2,0:T(2,128)}, u32[]{:S(2)}) copy-start(s32[2,16,2]{1,2,0:T(2,128)} %param.15) | copy-start | bytes 772
  21.1 5.7 copy-start.1
  38.7 79.9 %copy-start = (bf16[384,256]{1,0:T(8,128)(2,1)S(1)}, bf16[384,256]{1,0:T(8,128)(2,1)}, u32[]{:S(2)}) copy-start(bf16[384,256]{1,0:T(8,128)(2,1)} %param.14) | copy-start | bytes 589828
  41.0 811.9 %reduce-scatter.2.cloned.1.call-start = ((), (), s32[]{:S(2)}) async-start(), calls=%async_computation.2 | async-start | bytes 7864320 | tf_op jit(solution)/shard_map/reduce_scatter | solution.py:30
Sparse Core Ops, SparseCore 0:
  11.8 106.7 all-gather.1
  128.4 76.1 reduce-scatter.1
Sparse Core Ops, SparseCore 1:
  41.1 811.7 all-reduce.1
where the time goes:
time: 863 us; the launch traced here: 862 us
  waiting for transfers between devices  793 us (92%)
  local copies, waits for them, and re-layouts  20.1 us (2%)
  matrix products  19.1 us (2%)
  between operations  15.6 us (2%)
  other arithmetic  14.5 us (2%)
    psum x1, waiting for transfers between devices, local(): block_grads = lax.psum(local_grads, ('fsdp', 'replica'))  715 us
    all_gather x1, waiting for transfers between devices, local(): shard_rows = lax.all_gather(stacked, 'fsdp', axis=0, tiled=True)  77.6 us
  transfers between devices with their start and end apart: 3, of which 2 were waited for; matrix products, arithmetic and copies ran while one was open for 6% of the time, Pallas kernels for 0%

commit v1 on v0

--- a/solution.py
+++ b/solution.py
@@ -45,7 +45,7 @@
         "tbi,tbj->bij", left_blocks, right_blocks, preferred_element_type=jnp.float32
     )
     local_grads = local_grads.reshape(2, blocks.shape[1], BLK * BLK)
-    block_grads = lax.psum(local_grads, ("fsdp", "replica"))
+    block_grads = lax.psum(lax.psum(local_grads, "fsdp"), "replica")
     return (key_out, value_out, normed_grad, block_grads)
 
 

time: 863 us -> 455 us (0.53)
  waiting for transfers between devices: 793 us -> 383 us
    psum x1 -> x2, waiting for transfers between devices: 715 us -> 208 us  [local(): block_grads = lax.psum(lax.psum(local_grads, 'fsdp'), 'replica')]
    reduce_scatter x1, waiting for transfers between devices: 0.01 us -> 69.9 us  [local(): lax.psum_scatter(partial_value, 'tensor', scatter_dimension=1, tiled=True)]
    all_gather x1, waiting for transfers between devices: 77.6 us -> 105 us  [local(): shard_rows = lax.all_gather(stacked, 'fsdp', axis=0, tiled=True)]
  transfers between devices with their start and end apart: 3 -> 4, of which waited for: 2 -> 4; matrix products, arithmetic and copies ran while one was open for 6% -> 5% of each run, Pallas kernels for 0% -> 0%
where the time goes in v1:
time: 455 us; the launch traced here: 453 us
  waiting for transfers between devices  383 us (84%)
  local copies, waits for them, and re-layouts  20.6 us (5%)
  matrix products  20.2 us (4%)
  other arithmetic  15.1 us (3%)
  between operations  13.9 us (3%)
    psum x2, waiting for transfers between devices, local(): block_grads = lax.psum(lax.psum(local_grads, 'fsdp'), 'replica')  208 us
    all_gather x1, waiting for transfers between devices, local(): shard_rows = lax.all_gather(stacked, 'fsdp', axis=0, tiled=True)  105 us
    reduce_scatter x1, waiting for transfers between devices, local(): lax.psum_scatter(partial_value, 'tensor', scatter_dimension=1, tiled=True)  69.9 us
    unnamed x10, local copies, waits for them, and re-layouts  12.8 us
    dot_general x1, matrix products, local(): lax.dot_general(cot_both, whole, contract_cols, preferred_element_type=jn...  10.9 us
  transfers between devices with their start and end apart: 4, of which 4 were waited for; matrix products, arithmetic and copies ran while one was open for 5% of the time, Pallas kernels for 0%

profile of v1, /device:TPU:8, one launch (start us, length us, event | category | flops | bytes accessed | tf_op | source)
XLA Modules:
  0.0 453.1 jit_solution(15159295318665513667)
XLA Ops:
  7.2 0.0 all-reduce.3.cloned.1.call-start
  7.2 0.7 compare_and_fusion.1
  7.9 0.7 slice_reduce_fusion
  8.6 1.1 copy.12
  9.7 1.1 copy.13
  10.8 8.7 %copy.11 = bf16[384,8192]{0,1:T(8,128)(2,1)} copy(bf16[384,8192]{1,0:T(8,128)(2,1)} %param.9) | data formatting | bytes 12582912 | tf_op args[0]
  19.5 4.2 fusion
  23.7 0.1 reshape_squeeze.6
  23.8 0.1 reshape_squeeze.5
  23.9 0.7 gather_fusion.1
  24.6 0.7 gather_fusion.2
  25.4 8.0 %fusion.2 = bf16[384,8192]{0,1:T(8,128)(2,1)} fusion(bf16[384,8192]{0,1:T(8,128)(2,1)} %copy.11, f32[8192]{0:T(1024)S(1)} %copy-done.2, f32[384]{0:T(512)S(1)} %add_rsqrt_fusion), kind=kLoop, calls=%fused_computation.7 | loop fusion | flops 12582912 | bytes 12617216 | tf_op jit(solution)/shard_map/convert_element_type | solution.py:16
  33.4 3.7 gather_fusion
  37.1 0.2 select_bitcast_fusion
  37.4 0.8 fusion.3
  38.1 1.2 reshape.75
  39.3 0.0 all-reduce.3.cloned.1.call-update
  39.3 0.0 all-gather.2.cloned.1.call-start
  39.4 1.9 pad_maximum_fusion
  41.2 0.0 all-gather.2.cloned.1.call-update
  41.3 0.0 all-reduce.5.cloned.1.call-start
  41.3 167.0 %all-reduce.3.cloned.1.call-done = f32[2,16,4096]{2,1,0:T(8,128)} async-done(((f32[2,16,4096]{2,1,0:T(8,128)}), f32[2,16,4096]{2,1,0:T(8,128)}) %all-reduce.3.cloned.1.call-update) | async-done | bytes 524304 | tf_op jit(solution)/shard_map/psum | solution.py:48
  208.3 0.0 all-reduce.5.cloned.1.call-update
  208.3 0.0 reduce-scatter.2.cloned.1.call-start
  208.4 105.0 %all-gather.2.cloned.1.call-done = bf16[8192,512]{1,0:T(8,128)(2,1)} async-done(((bf16[512,512]{1,0:T(8,128)(2,1)}), bf16[8192,512]{1,0:T(8,128)(2,1)}) %all-gather.2.cloned.1.call-update) | async-done | bytes 8388624 | tf_op jit(solution)/shard_map/all_gather | solution.py:20
  313.4 10.9 %convolution_convert_fusion = bf16[384,8192]{1,0:T(8,128)(2,1)} fusion(bf16[8192,512]{1,0:T(8,128)(2,1)} %all-gather.2.cloned.1.call-done, bf16[384,256]{1,0:T(8,128)(2,1)S(1)} %copy-done, bf16[384,256]{1,0:T(8,128)(2,1)S(1)} %copy-done.1), kind=kOutput, calls=%fused_computation.8 | convolution fusion | flops 3225157632 | bytes 15073280 | tf_op jit(solution)/shard_map/dot_general | solution.py:24
  324.2 0.0 reduce-scatter.2.cloned.1.call-update
  324.2 8.6 %convolution_convert_fusion.1 = bf16[384,512]{1,0:T(8,128)(2,1)S(1)} fusion(bf16[384,8192]{0,1:T(8,128)(2,1)} %fusion.2, bf16[8192,512]{1,0:T(8,128)(2,1)} %all-gather.2.cloned.1.call-done), kind=kOutput, calls=%fused_computation.16 | convolution fusion | flops 3221422080 | bytes 15073280 | tf_op jit(solution)/shard_map/dot_general | solution.py:21
  332.9 0.8 fusion.18
  333.6 41.2 %all-reduce.5.cloned.1.call-done = f32[2,16,4096]{2,1,0:T(8,128)} async-done(((f32[2,16,4096]{2,1,0:T(8,128)}), f32[2,16,4096]{2,1,0:T(8,128)}) %all-reduce.5.cloned.1.call-update) | async-done | bytes 524304 | tf_op jit(solution)/shard_map/psum | solution.py:48
  374.8 69.9 %reduce-scatter.2.cloned.1.call-done = bf16[384,2048]{1,0:T(8,128)(2,1)} async-done(((bf16[384,8192]{1,0:T(8,128)(2,1)}), bf16[384,2048]{1,0:T(8,128)(2,1)}) %reduce-scatter.2.cloned.1.call-update) | async-done | bytes 1572880 | tf_op jit(solution)/shard_map/reduce_scatter | solution.py:30
  444.7 1.9 copy.16
  (12 shorter events, 0.1 us)
Async XLA Ops:
  7.2 201.2 %all-reduce.3.cloned.1.call-start = ((), (), s32[]{:S(2)}) async-start(), calls=%async_computation.3 | async-start | bytes 1048576 | tf_op jit(solution)/shard_map/psum | solution.py:48
  19.5 5.9 %copy-start.2 = (f32[8192]{0:T(1024)S(1)}, f32[8192]{0:T(1024)}, u32[]{:S(2)}) copy-start(f32[8192]{0:T(1024)} %param.10) | copy-start | bytes 98308
  37.4 276.0 %copy-start = (bf16[384,256]{1,0:T(8,128)(2,1)S(1)}, bf16[384,256]{1,0:T(8,128)(2,1)}, u32[]{:S(2)}) copy-start(bf16[384,256]{1,0:T(8,128)(2,1)} %param.14) | copy-start | bytes 589828
  37.4 276.0 %copy-start.1 = (bf16[384,256]{1,0:T(8,128)(2,1)S(1)}, bf16[384,256]{1,0:T(8,128)(2,1)}, u32[]{:S(2)}) copy-start(bf16[384,256]{1,0:T(8,128)(2,1)} %param.13) | copy-start | bytes 589828
  39.3 274.0 %all-gather.2.cloned.1.call-start = ((), (), s32[]{:S(2)}) async-start(), calls=%async_computation.1 | async-start | bytes 8912896 | tf_op jit(solution)/shard_map/all_gather | solution.py:20
  41.3 333.6 %all-reduce.5.cloned.1.call-start = ((), (), s32[]{:S(2)}) async-start(), calls=%async_computation.4 | async-start | bytes 1048576 | tf_op jit(solution)/shard_map/psum | solution.py:48
  208.3 236.4 %reduce-scatter.2.cloned.1.call-start = ((), (), s32[]{:S(2)}) async-start(), calls=%async_computation.2 | async-start | bytes 7864320 | tf_op jit(solution)/shard_map/reduce_scatter | solution.py:30
Sparse Core Ops, SparseCore 0:
  39.4 168.8 all-reduce.2
  211.6 101.6 all-gather.1
  315.8 58.9 all-reduce.4
  378.0 66.6 reduce-scatter.1

commit v2 on v0

--- a/solution.py
+++ b/solution.py
@@ -45,7 +45,7 @@
         "tbi,tbj->bij", left_blocks, right_blocks, preferred_element_type=jnp.float32
     )
     local_grads = local_grads.reshape(2, blocks.shape[1], BLK * BLK)
-    block_grads = lax.psum(local_grads, ("fsdp", "replica"))
+    block_grads = jnp.sum(lax.all_gather(local_grads, ("fsdp", "replica")), axis=0)
     return (key_out, value_out, normed_grad, block_grads)
 
 

time: 863 us -> 494 us (0.57)
  waiting for transfers between devices: 793 us -> 414 us
  other arithmetic: 14.5 us -> 27 us
    psum x1 -> x0, waiting for transfers between devices: 715 us -> none  [local(): block_grads = lax.psum(local_grads, ('fsdp', 'replica'))]
    all_gather x0 -> x1, waiting for transfers between devices: none -> 282 us  [local(): lax.all_gather(local_grads, ('fsdp', 'replica'))]
    reduce_scatter x1, waiting for transfers between devices: 0.01 us -> 55.4 us  [local(): lax.psum_scatter(partial_value, 'tensor', scatter_dimension=1, tiled=True)]
    reduce_sum x0 -> x1, other arithmetic: none -> 12.5 us  [local(): jnp.sum(lax.all_gather(local_grads, ('fsdp', 'replica')), axis=0)]
  transfers between devices with their start and end apart: 3 -> 3, of which waited for: 2 -> 3; matrix products, arithmetic and copies ran while one was open for 6% -> 13% of each run, Pallas kernels for 0% -> 0%
where the time goes in v2:
time: 494 us; the launch traced here: 493 us
  waiting for transfers between devices  414 us (84%)
  other arithmetic  27 us (5%)
  matrix products  19.2 us (4%)
  local copies, waits for them, and re-layouts  18.9 us (4%)
  between operations  13.9 us (3%)
    all_gather x1, waiting for transfers between devices, local(): lax.all_gather(local_grads, ('fsdp', 'replica'))  282 us
    all_gather x1, waiting for transfers between devices, local(): shard_rows = lax.all_gather(stacked, 'fsdp', axis=0, tiled=True)  76.1 us
    reduce_scatter x1, waiting for transfers between devices, local(): lax.psum_scatter(partial_value, 'tensor', scatter_dimension=1, tiled=True)  55.4 us
    reduce_sum x1, other arithmetic, local(): jnp.sum(lax.all_gather(local_grads, ('fsdp', 'replica')), axis=0)  12.5 us
    unnamed x7, local copies, waits for them, and re-layouts  10.9 us
  transfers between devices with their start and end apart: 3, of which 3 were waited for; matrix products, arithmetic and copies ran while one was open for 13% of the time, Pallas kernels for 0%

profile of v2, /device:TPU:8, one launch (start us, length us, event | category | flops | bytes accessed | tf_op | source)
XLA Modules:
  0.0 492.7 jit_solution(14232964200704546445)
XLA Ops:
  7.2 0.0 all-gather.3.cloned.1.call-start
  7.2 1.9 pad_maximum_fusion
  9.1 0.0 all-gather.3.cloned.1.call-update
  9.1 0.0 all-gather.5.cloned.1.call-start
  9.1 0.7 slice_reduce_fusion
  9.8 0.1 reshape_squeeze.5
  9.9 0.1 reshape_squeeze.6
  10.0 1.1 copy.15
  11.1 1.1 copy.16
  12.2 0.0 copy-start.1
  12.2 8.7 %copy.14 = bf16[384,8192]{0,1:T(8,128)(2,1)} copy(bf16[384,8192]{1,0:T(8,128)(2,1)} %param.9) | data formatting | bytes 12582912 | tf_op args[0]
  20.9 0.0 copy-done.1
  20.9 0.0 copy-start
  20.9 0.7 gather_fusion.2
  21.7 0.7 gather_fusion.1
  22.4 4.2 fusion
  26.6 0.0 copy-done
  26.6 8.2 %fusion.2 = bf16[384,8192]{0,1:T(8,128)(2,1)} fusion(bf16[384,8192]{0,1:T(8,128)(2,1)} %copy.14, f32[8192]{0:T(1024)S(1)} %copy-done, f32[384]{0:T(512)S(1)} %add_rsqrt_fusion), kind=kLoop, calls=%fused_computation.7 | loop fusion | flops 12582912 | bytes 12617216 | tf_op jit(solution)/shard_map/convert_element_type | solution.py:16
  34.8 3.8 gather_fusion
  38.6 0.2 select_bitcast_fusion
  38.9 0.8 fusion.3
  39.7 1.2 all_gather_reshape.3
  40.8 0.0 all-gather.5.cloned.1.call-update
  40.9 0.0 reduce-scatter.2.cloned.1.call-start
  40.9 76.1 %all-gather.3.cloned.1.call-done = bf16[8192,512]{1,0:T(8,128)(2,1)} async-done(((bf16[512,512]{1,0:T(8,128)(2,1)}), bf16[8192,512]{1,0:T(8,128)(2,1)}) %all-gather.3.cloned.1.call-update) | async-done | bytes 8388624 | tf_op jit(solution)/shard_map/all_gather | solution.py:20
  117.0 9.8 %convolution_convert_fusion = bf16[384,8192]{1,0:T(8,128)(2,1)} fusion(bf16[8192,512]{1,0:T(8,128)(2,1)} %all-gather.3.cloned.1.call-done, bf16[384,256]{1,0:T(8,128)(2,1)} %param.14, bf16[384,256]{1,0:T(8,128)(2,1)} %param.13), kind=kOutput, calls=%fused_computation.8 | convolution fusion | flops 3225157632 | bytes 15073280 | tf_op jit(solution)/shard_map/dot_general | solution.py:24
  126.8 0.0 reduce-scatter.2.cloned.1.call-update
  126.8 8.6 %convolution_convert_fusion.1 = bf16[384,512]{1,0:T(8,128)(2,1)S(1)} fusion(bf16[384,8192]{0,1:T(8,128)(2,1)} %fusion.2, bf16[8192,512]{1,0:T(8,128)(2,1)} %all-gather.3.cloned.1.call-done), kind=kOutput, calls=%fused_computation.16 | convolution fusion | flops 3221422080 | bytes 15073280 | tf_op jit(solution)/shard_map/dot_general | solution.py:21
  135.4 0.8 fusion.18
  136.2 282.1 %all-gather.5.cloned.1.call-done = f32[64,2,16,4096]{3,2,1,0:T(8,128)} async-done(((f32[1,2,16,4096]{3,2,1,0:T(8,128)}), f32[64,2,16,4096]{3,2,1,0:T(8,128)}) %all-gather.5.cloned.1.call-update) | async-done | bytes 33554448 | tf_op jit(solution)/shard_map/all_gather | solution.py:48
  418.3 12.5 %reduce_sum.19 = f32[2,16,4096]{2,1,0:T(8,128)} reduce(f32[64,2,16,4096]{3,2,1,0:T(8,128)} %all-gather.5.cloned.1.call-done, f32[]{:T(128)} %constant.17.clone.1), dimensions={0}, to_apply=%region_2.0 | reduce | flops 8257536 | bytes 34078724 | tf_op jit(solution)/shard_map/reduce_sum | solution.py:48
  430.8 55.4 %reduce-scatter.2.cloned.1.call-done = bf16[384,2048]{1,0:T(8,128)(2,1)} async-done(((bf16[384,8192]{1,0:T(8,128)(2,1)}), bf16[384,2048]{1,0:T(8,128)(2,1)}) %reduce-scatter.2.cloned.1.call-update) | async-done | bytes 1572880 | tf_op jit(solution)/shard_map/reduce_scatter | solution.py:30
  (7 shorter events, 0.0 us)
Async XLA Ops:
  7.2 109.8 %all-gather.3.cloned.1.call-start = ((), (), s32[]{:S(2)}) async-start(), calls=%async_computation.1 | async-start | bytes 8912896 | tf_op jit(solution)/shard_map/all_gather | solution.py:20
  9.1 409.2 %all-gather.5.cloned.1.call-start = ((), (), s32[]{:S(2)}) async-start(), calls=%async_computation.3 | async-start | bytes 34078720 | tf_op jit(solution)/shard_map/all_gather | solution.py:48
  12.2 8.7 %copy-start.1 = (s32[2,16,2]{1,2,0:T(2,128)S(1)}, s32[2,16,2]{1,2,0:T(2,128)}, u32[]{:S(2)}) copy-start(s32[2,16,2]{1,2,0:T(2,128)} %param.15) | copy-start | bytes 772
  20.9 5.7 %copy-start = (f32[8192]{0:T(1024)S(1)}, f32[8192]{0:T(1024)}, u32[]{:S(2)}) copy-start(f32[8192]{0:T(1024)} %param.10) | copy-start | bytes 98308
  40.9 445.3 %reduce-scatter.2.cloned.1.call-start = ((), (), s32[]{:S(2)}) async-start(), calls=%async_computation.2 | async-start | bytes 7864320 | tf_op jit(solution)/shard_map/reduce_scatter | solution.py:30
Sparse Core Ops, SparseCore 0:
  11.0 105.9 all-gather.2
  120.3 297.9 all-gather.4
  421.5 64.6 reduce-scatter.1
